TPU v7x, 32 devices: a whole 2x2x4 slice. The times are simulated.
32 devices in a mesh: sector: 8 (over y, x, core), term: 4 (over z).
Axes of the slice: x: 2, y: 2, z: 4, core: 2. Of those that a mesh axis runs over, the one named last changes fastest.
Arguments:
- wave: float32 [8, 512, 512], P('sector', 'term'), may hold values from -12 to 12
- left_ops: bfloat16 [16, 8, 512, 512], P('term', 'sector'), may hold values from -4 to 4
- right_ops: bfloat16 [16, 8, 512, 512], P('term', 'sector'), may hold values from -4 to 4
- charges: int32 [16], replicated, may hold values from -1 to 1, as said below
- diag: float32 [8, 512, 512], P('sector', 'term'), may hold values from 0.5 to 8
Outputs:
- psi_out: float32 [8, 512, 512], P('sector', 'term')
Inputs may be any that keep to these rules, and one draw needn't show every extreme that they name: `charges`: exactly (17) // 2 terms have charge 0; at least one term has charge 1 and at least one has charge -1.
All inputs are finite; a program needn't handle non-finite values.
Results may differ from a plain program's by a relative error of at most 0.0085.
Values may be sent and summed in bfloat16 or wider, within the bound.
No kernel may reach another device: no remote copies, remote signals or barrier semaphores. Data moves between devices by JAX's collectives and lax.ppermute only.
A program may use at most 64 MiB of HBM per device.

v0:
```python
import jax
import jax.numpy as jnp
from jax import lax
from jax.sharding import PartitionSpec as P

STEPS = 3


def from_behind(value, axis, steps):
    count = lax.axis_size(axis)
    leading, last = (max(0, -steps), min(count, count - steps))
    return lax.ppermute(value, axis, [(source, source + steps) for source in range(leading, last)])


def apply_terms(left_ops, right_ops, my_charges, own, lower, upper):
    stacked = jnp.stack([upper, own, lower])
    picked = stacked[my_charges + 1]
    inner = jnp.einsum(
        "tij,tjk->tik", left_ops[:, 0], picked, preferred_element_type=jnp.float32
    ).astype(jnp.bfloat16)
    image = jnp.einsum("tij,tkj->tik", inner, right_ops[:, 0], preferred_element_type=jnp.float32)
    return jnp.sum(image, axis=0)


def per_device(wave, left_ops, right_ops, charges, diag):
    per_dev = left_ops.shape[0]
    my_charges = lax.dynamic_slice_in_dim(charges, lax.axis_index("term") * per_dev, per_dev)
    psi, full_diag = (
        lax.all_gather(wave[0], "term", axis=0, tiled=True),
        lax.all_gather(diag[0], "term", axis=0, tiled=True),
    )
    for step in range(STEPS):
        wb = psi.astype(jnp.bfloat16)
        lower = from_behind(wb, "sector", 1)
        upper = from_behind(wb, "sector", -1)
        partial_image = apply_terms(left_ops, right_ops, my_charges, wb, lower, upper)
        hpsi = lax.psum(partial_image, "term")
        cross, square = lax.psum((jnp.sum(psi * hpsi), jnp.sum(psi * psi)), "sector")
        theta = cross / square
        fresh = psi - (hpsi - theta * psi) / jnp.maximum(jnp.abs(full_diag - theta), 1.0)
        total = lax.psum(jnp.sum(fresh * fresh), "sector")
        psi = fresh / jnp.sqrt(total / (lax.axis_size("sector") * fresh.size) + 1e-06)
    rows_dev = wave.shape[1]
    result = lax.dynamic_slice_in_dim(psi, lax.axis_index("term") * rows_dev, rows_dev, 0)
    return result[None]


def solution(mesh):
    in_specs = (
        P("sector", "term", None),
        P("term", "sector", None, None),
        P("term", "sector", None, None),
        P(),
        P("sector", "term", None),
    )
    out_specs = P("sector", "term", None)
    return jax.shard_map(
        per_device, mesh=mesh, in_specs=in_specs, out_specs=out_specs, check_vma=False
    )
```

profile of v0, /device:TPU:0, one launch (start us, length us, event | category | flops | bytes accessed | tf_op | source)
XLA Modules:
  0.0 397.1 jit_solution(17423861717904664301)
XLA Ops:
  7.3 32.3 %all-gather.5.cloned.1.call-done = f32[1,512,512]{2,1,0:T(8,128)} async-done(((f32[1,128,512]{2,1,0:T(8,128)}), f32[1,512,512]{2,1,0:T(8,128)}) %all-gather.5.cloned.1.call-update) | async-done | bytes 1048592 | tf_op jit(solution)/shard_map/all_gather | solution.py:29
  46.0 2.9 collective-permute-done
  49.0 2.5 pad_maximum_fusion
  51.5 3.4 gather_fusion
  54.9 5.5 %fusion.30 = f32[512,512]{1,0:T(8,128)} fusion(bf16[4,1,512,512]{3,2,1,0:T(8,128)(2,1)S(1)} %copy-done, bf16[4,512,512]{2,1,0:T(8,128)(2,1)} %gather_fusion, bf16[4,1,512,512]{3,2,1,0:T(8,128)(2,1)} %param.6), kind=kOutput, calls=%fused_computation.24 | convolution fusion | flops 2148532224 | bytes 7340032 | tf_op jit(solution)/shard_map/tij,tkj->tik/dot_general | solution.py:21
  61.3 59.4 %all-reduce.7.cloned.1.call-done = f32[512,512]{1,0:T(8,128)} async-done(((f32[512,512]{1,0:T(8,128)}), f32[512,512]{1,0:T(8,128)}) %all-reduce.7.cloned.1.call-update) | async-done | bytes 1048592 | tf_op jit(solution)/shard_map/psum | solution.py:37
  122.8 14.7 %all-reduce.2 = (f32[]{:T(128)}, f32[]{:T(128)}) all-reduce(f32[]{:T(128)} %get-tuple-element.10, f32[]{:T(128)} %get-tuple-element.9), channel_id=1, replica_groups=mesh['sector'=8,'term'=4] {'sector'}, use_global_device_ids=true, to_apply=%region_2.0 | all-reduce | flops 2 | bytes 16 | tf_op jit(solution)/shard_map/psum | solution.py:38
  138.8 10.7 %all-gather.7.cloned.1.call-done = f32[1,512,512]{2,1,0:T(8,128)} async-done(((f32[1,128,512]{2,1,0:T(8,128)}), f32[1,512,512]{2,1,0:T(8,128)}) %all-gather.7.cloned.1.call-update) | async-done | bytes 1048592 | tf_op jit(solution)/shard_map/all_gather | solution.py:30
  149.5 2.8 multiply_reduce_fusion.6
  152.4 13.7 %psum.87 = f32[]{:T(128)} all-reduce(f32[]{:T(128)} %get-tuple-element.21), channel_id=1, replica_groups=mesh['sector'=8,'term'=4] {'sector'}, use_global_device_ids=true, to_apply=%region_6.0 | all-reduce | flops 1 | bytes 8 | tf_op jit(solution)/shard_map/psum | solution.py:41
  169.7 2.3 collective-permute-done.2
  173.4 3.4 gather_fusion.1
  176.8 5.5 %fusion.37 = f32[512,512]{1,0:T(8,128)} fusion(bf16[4,1,512,512]{3,2,1,0:T(8,128)(2,1)S(1)} %copy-done, bf16[4,512,512]{2,1,0:T(8,128)(2,1)} %gather_fusion.1, bf16[4,1,512,512]{3,2,1,0:T(8,128)(2,1)} %param.6), kind=kOutput, calls=%fused_computation.25 | convolution fusion | flops 2148532224 | bytes 7340032 | tf_op jit(solution)/shard_map/tij,tkj->tik/dot_general | solution.py:21
  182.4 60.9 %all-reduce.9.cloned.1.call-done = f32[512,512]{1,0:T(8,128)} async-done(((f32[512,512]{1,0:T(8,128)}), f32[512,512]{1,0:T(8,128)}) %all-reduce.9.cloned.1.call-update) | async-done | bytes 1048592 | tf_op jit(solution)/shard_map/psum | solution.py:37
  245.5 14.3 %all-reduce.1 = (f32[]{:T(128)}, f32[]{:T(128)}) all-reduce(f32[]{:T(128)} %get-tuple-element.8, f32[]{:T(128)} %get-tuple-element.7), channel_id=1, replica_groups=mesh['sector'=8,'term'=4] {'sector'}, use_global_device_ids=true, to_apply=%region_9.0 | all-reduce | flops 2 | bytes 16 | tf_op jit(solution)/shard_map/psum | solution.py:38
  261.1 3.6 multiply_reduce_fusion.3
  264.6 12.4 %psum.91 = f32[]{:T(128)} all-reduce(f32[]{:T(128)} %get-tuple-element.19), channel_id=1, replica_groups=mesh['sector'=8,'term'=4] {'sector'}, use_global_device_ids=true, to_apply=%region_13.0 | all-reduce | flops 1 | bytes 8 | tf_op jit(solution)/shard_map/psum | solution.py:41
  282.4 2.3 collective-permute-done.4
  286.0 3.4 gather_fusion.2
  289.5 5.5 %fusion.44 = f32[512,512]{1,0:T(8,128)} fusion(bf16[4,1,512,512]{3,2,1,0:T(8,128)(2,1)S(1)} %copy-done, bf16[4,512,512]{2,1,0:T(8,128)(2,1)} %gather_fusion.2, bf16[4,1,512,512]{3,2,1,0:T(8,128)(2,1)} %param.6), kind=kOutput, calls=%fused_computation.26 | convolution fusion | flops 2148532224 | bytes 7340032 | tf_op jit(solution)/shard_map/tij,tkj->tik/dot_general | solution.py:21
  295.0 59.5 %all-reduce.11.cloned.1.call-done = f32[512,512]{1,0:T(8,128)} async-done(((f32[512,512]{1,0:T(8,128)}), f32[512,512]{1,0:T(8,128)}) %all-reduce.11.cloned.1.call-update) | async-done | bytes 1048592 | tf_op jit(solution)/shard_map/psum | solution.py:37
  356.7 14.3 %all-reduce = (f32[]{:T(128)}, f32[]{:T(128)}) all-reduce(f32[]{:T(128)} %get-tuple-element.6, f32[]{:T(128)} %get-tuple-element.5), channel_id=1, replica_groups=mesh['sector'=8,'term'=4] {'sector'}, use_global_device_ids=true, to_apply=%region_16.0 | all-reduce | flops 2 | bytes 16 | tf_op jit(solution)/shard_map/psum | solution.py:38
  372.3 3.6 multiply_reduce_fusion
  375.8 12.4 %psum.95 = f32[]{:T(128)} all-reduce(f32[]{:T(128)} %get-tuple-element.17), channel_id=1, replica_groups=mesh['sector'=8,'term'=4] {'sector'}, use_global_device_ids=true, to_apply=%region_20.0 | all-reduce | flops 1 | bytes 8 | tf_op jit(solution)/shard_map/psum | solution.py:41
  (39 shorter events, 26.4 us)
Async XLA Ops:
  6.5 48.4 %copy-start = (bf16[4,1,512,512]{3,2,1,0:T(8,128)(2,1)S(1)}, bf16[4,1,512,512]{3,2,1,0:T(8,128)(2,1)}, u32[]{:S(2)}) copy-start(bf16[4,1,512,512]{3,2,1,0:T(8,128)(2,1)} %param.7) | copy-start | bytes 6291460
  6.5 33.1 %all-gather.5.cloned.1.call-start = ((), (), s32[]{:S(2)}) async-start(), calls=%async_computation.3 | async-start | bytes 1310720 | tf_op jit(solution)/shard_map/all_gather | solution.py:29
  7.3 113.4 %all-reduce.7.cloned.1.call-start = ((), (), s32[]{:S(2)}) async-start(), calls=%async_computation | async-start | bytes 2097152 | tf_op jit(solution)/shard_map/psum | solution.py:37
  39.6 6.3 %copy-start.2 = (f32[1,512,512]{2,1,0:T(8,128)S(1)}, f32[1,512,512]{2,1,0:T(8,128)}, u32[]{:S(2)}) copy-start(f32[1,512,512]{2,1,0:T(8,128)} %all-gather.5.cloned.1.call-done) | copy-start | bytes 3145732
  41.8 4.2 %collective-permute-start.1 = (bf16[512,512]{1,0:T(8,128)(2,1)}, bf16[512,512]{1,0:T(8,128)(2,1)}, u32[]{:S(2)}, u32[]{:S(2)}) collective-permute-start(bf16[512,512]{1,0:T(8,128)(2,1)} %bitcast_convert_fusion), channel_id=1, source_target_pairs={{0,4},{4,8},{8,12},{12,16},{16,20},{20,24},{24,28},{1,5},{5,9},{9,... | collective-permute-start | bytes 1572872 | tf_op jit(solution)/shard_map/ppermute | solution.py:12
  43.9 5.0 %collective-permute-start = (bf16[512,512]{1,0:T(8,128)(2,1)}, bf16[512,512]{1,0:T(8,128)(2,1)}, u32[]{:S(2)}, u32[]{:S(2)}) collective-permute-start(bf16[512,512]{1,0:T(8,128)(2,1)} %bitcast_convert_fusion), channel_id=1, source_target_pairs={{4,0},{8,4},{12,8},{16,12},{20,16},{24,20},{28,24},{5,1},{9,5},{13... | collective-permute-start | bytes 1572872 | tf_op jit(solution)/shard_map/ppermute | solution.py:12
  60.5 89.0 %all-gather.7.cloned.1.call-start = ((), (), s32[]{:S(2)}) async-start(), calls=%async_computation.4 | async-start | bytes 1310720 | tf_op jit(solution)/shard_map/all_gather | solution.py:30
  61.2 182.1 %all-reduce.9.cloned.1.call-start = ((), (), s32[]{:S(2)}) async-start(), calls=%async_computation.1 | async-start | bytes 2097152 | tf_op jit(solution)/shard_map/psum | solution.py:37
  166.9 2.8 collective-permute-start.3
  168.2 3.8 collective-permute-start.2
  182.4 172.1 %all-reduce.11.cloned.1.call-start = ((), (), s32[]{:S(2)}) async-start(), calls=%async_computation.2 | async-start | bytes 2097152 | tf_op jit(solution)/shard_map/psum | solution.py:37
  264.6 17.6 %copy-start.1 = (f32[512,512]{1,0:T(8,128)S(1)}, f32[512,512]{1,0:T(8,128)}, u32[]{:S(2)}) copy-start(f32[512,512]{1,0:T(8,128)} %get-tuple-element.20) | copy-start | bytes 3145732
  279.1 3.3 collective-permute-start.5
  280.9 3.8 collective-permute-start.4
Sparse Core Ops, SparseCore 0:
  8.9 30.6 all-gather.4
  60.6 59.9 all-reduce.6
  122.2 27.2 all-gather.6
  182.5 60.7 all-reduce.8
  295.2 59.3 all-reduce.10
where the time goes:
time: 398 us; the launch traced here: 397 us
  waiting for transfers between devices  232 us (58%)
  blocking collectives  81.9 us (21%)
  other arithmetic  28 us (7%)
  between operations  19.1 us (5%)
  matrix products  16.6 us (4%)
  local copies, waits for them, and re-layouts  10.3 us (3%)
  starting transfers between devices  9.25 us (2%)
    psum x3, waiting for transfers between devices, per_device(): hpsi = lax.psum(partial_image, 'term')  180 us
    psum x3, blocking collectives, per_device(): lax.psum((jnp.sum(psi * hpsi), jnp.sum(psi * psi)), 'sector')  43.4 us
    psum x3, blocking collectives, per_device(): total = lax.psum(jnp.sum(fresh * fresh), 'sector')  38.6 us
    all_gather x1, waiting for transfers between devices, per_device(): lax.all_gather(wave[0], 'term', axis=0, tiled=True)  32.3 us
    dot_general x3, matrix products, apply_terms(): jnp.einsum('tij,tkj->tik', inner, right_ops[:, 0], preferred_element_type...  16.6 us
    all_gather x1, waiting for transfers between devices, per_device(): lax.all_gather(diag[0], 'term', axis=0, tiled=True)  10.7 us
    gather x3, local copies, waits for them, and re-layouts, apply_terms(): picked = stacked[my_charges + 1]  10.3 us
    reduce_sum x3, other arithmetic, per_device(): total = lax.psum(jnp.sum(fresh * fresh), 'sector')  9.95 us
  transfers between devices with their start and end apart: 11, of which 10 were waited for; matrix products, arithmetic and copies ran while one was open for 1% of the time, Pallas kernels for 0%

commit v1 on v0

--- a/solution.py
+++ b/solution.py
@@ -34,7 +34,9 @@
         lower = from_behind(wb, "sector", 1)
         upper = from_behind(wb, "sector", -1)
         partial_image = apply_terms(left_ops, right_ops, my_charges, wb, lower, upper)
-        hpsi = lax.psum(partial_image, "term")
+        hpsi = partial_image
+        for hop in (1, 2):
+            hpsi = hpsi + lax.ppermute(hpsi, "term", [(dev, dev ^ hop) for dev in range(4)])
         cross, square = lax.psum((jnp.sum(psi * hpsi), jnp.sum(psi * psi)), "sector")
         theta = cross / square
         fresh = psi - (hpsi - theta * psi) / jnp.maximum(jnp.abs(full_diag - theta), 1.0)

time: 398 us -> 473 us (1.19)
  blocking collectives: 81.9 us -> 144 us
  other arithmetic: 28 us -> 34.5 us
    ppermute x0 -> x6, waiting for transfers between devices: none -> 188 us  [per_device(): lax.ppermute(hpsi, 'term', [(dev, dev ^ hop) for dev in range(4)])]
    psum x3 -> x0, waiting for transfers between devices: 180 us -> none  [per_device(): hpsi = lax.psum(partial_image, 'term')]
    psum x3, blocking collectives: 43.4 us -> 106 us  [per_device(): lax.psum((jnp.sum(psi * hpsi), jnp.sum(psi * psi)), 'sector')]
    all_gather x1, waiting for transfers between devices: 10.7 us -> 0.02 us  [per_device(): lax.all_gather(diag[0], 'term', axis=0, tiled=True)]
    add x0 -> x3, other arithmetic: none -> 5.6 us  [per_device(): hpsi + lax.ppermute(hpsi, 'term', [(dev, dev ^ hop) for dev in range(4)])]
  transfers between devices with their start and end apart: 11 -> 14, of which waited for: 10 -> 12; matrix products, arithmetic and copies ran while one was open for 1% -> 1% of each run, Pallas kernels for 0% -> 0%
where the time goes in v1:
time: 473 us; the launch traced here: 471 us
  waiting for transfers between devices  232 us (49%)
  blocking collectives  144 us (30%)
  other arithmetic  34.5 us (7%)
  between operations  19.4 us (4%)
  matrix products  16.6 us (4%)
  starting transfers between devices  13.8 us (3%)
  local copies, waits for them, and re-layouts  10.3 us (2%)
    ppermute x6, waiting for transfers between devices, per_device(): lax.ppermute(hpsi, 'term', [(dev, dev ^ hop) for dev in range(4)])  188 us
    psum x3, blocking collectives, per_device(): lax.psum((jnp.sum(psi * hpsi), jnp.sum(psi * psi)), 'sector')  106 us
    psum x3, blocking collectives, per_device(): total = lax.psum(jnp.sum(fresh * fresh), 'sector')  37.2 us
    all_gather x1, waiting for transfers between devices, per_device(): lax.all_gather(wave[0], 'term', axis=0, tiled=True)  32.3 us
    dot_general x3, matrix products, apply_terms(): jnp.einsum('tij,tkj->tik', inner, right_ops[:, 0], preferred_element_type...  16.6 us
    ppermute x6, waiting for transfers between devices, from_behind(): lax.ppermute(value, axis, [(source, source + steps) for source in range(l...  11.2 us
    gather x3, local copies, waits for them, and re-layouts, apply_terms(): picked = stacked[my_charges + 1]  10.3 us
    reduce_sum x3, other arithmetic, per_device(): total = lax.psum(jnp.sum(fresh * fresh), 'sector')  9.91 us
  transfers between devices with their start and end apart: 14, of which 12 were waited for; matrix products, arithmetic and copies ran while one was open for 1% of the time, Pallas kernels for 0%

profile of v1, /device:TPU:0, one launch (start us, length us, event | category | flops | bytes accessed | tf_op | source)
XLA Modules:
  0.0 470.5 jit_solution(8344239694255216314)
XLA Ops:
  7.3 32.3 %all-gather.5.cloned.1.call-done = f32[1,512,512]{2,1,0:T(8,128)} async-done(((f32[1,128,512]{2,1,0:T(8,128)}), f32[1,512,512]{2,1,0:T(8,128)}) %all-gather.5.cloned.1.call-update) | async-done | bytes 1048592 | tf_op jit(solution)/shard_map/all_gather | solution.py:29
  51.5 3.4 gather_fusion
  54.9 5.5 %fusion.30 = f32[512,512]{1,0:T(8,128)} fusion(bf16[4,1,512,512]{3,2,1,0:T(8,128)(2,1)S(1)} %copy-done, bf16[4,512,512]{2,1,0:T(8,128)(2,1)} %gather_fusion, bf16[4,1,512,512]{3,2,1,0:T(8,128)(2,1)} %param.6), kind=kOutput, calls=%fused_computation.24 | convolution fusion | flops 2148532224 | bytes 7340032 | tf_op jit(solution)/shard_map/tij,tkj->tik/dot_general | solution.py:21
  61.9 15.8 %collective-permute-done.2 = f32[512,512]{1,0:T(8,128)} collective-permute-done((f32[512,512]{1,0:T(8,128)}, f32[512,512]{1,0:T(8,128)}, u32[]{:S(2)}, u32[]{:S(2)}) %collective-permute-start.2) | collective-permute-done | bytes 1048608 | tf_op jit(solution)/shard_map/ppermute | solution.py:39
  81.4 54.8 %collective-permute-done.3 = f32[512,512]{1,0:T(8,128)S(1)} collective-permute-done((f32[512,512]{1,0:T(8,128)S(1)}, f32[512,512]{1,0:T(8,128)S(1)}, u32[]{:S(2)}, u32[]{:S(2)}) %collective-permute-start.3) | collective-permute-done | bytes 1048608 | tf_op jit(solution)/shard_map/ppermute | solution.py:39
  138.3 35.9 %all-reduce.2 = (f32[]{:T(128)}, f32[]{:T(128)}) all-reduce(f32[]{:T(128)} %get-tuple-element.10, f32[]{:T(128)} %get-tuple-element.9), channel_id=1, replica_groups=mesh['sector'=8,'term'=4] {'sector'}, use_global_device_ids=true, to_apply=%region_1.0 | all-reduce | flops 2 | bytes 16 | tf_op jit(solution)/shard_map/psum | solution.py:40
  178.3 12.4 %psum.65 = f32[]{:T(128)} all-reduce(f32[]{:T(128)} %get-tuple-element.23), channel_id=1, replica_groups=mesh['sector'=8,'term'=4] {'sector'}, use_global_device_ids=true, to_apply=%region_5.0 | all-reduce | flops 1 | bytes 8 | tf_op jit(solution)/shard_map/psum | solution.py:43
  194.8 4.1 collective-permute-done.4
  200.3 3.4 gather_fusion.1
  203.7 5.5 %fusion.37 = f32[512,512]{1,0:T(8,128)} fusion(bf16[4,1,512,512]{3,2,1,0:T(8,128)(2,1)S(1)} %copy-done, bf16[4,512,512]{2,1,0:T(8,128)(2,1)} %gather_fusion.1, bf16[4,1,512,512]{3,2,1,0:T(8,128)(2,1)} %param.6), kind=kOutput, calls=%fused_computation.25 | convolution fusion | flops 2148532224 | bytes 7340032 | tf_op jit(solution)/shard_map/tij,tkj->tik/dot_general | solution.py:21
  209.2 15.0 %collective-permute-done.6 = f32[512,512]{1,0:T(8,128)S(1)} collective-permute-done((f32[512,512]{1,0:T(8,128)}, f32[512,512]{1,0:T(8,128)S(1)}, u32[]{:S(2)}, u32[]{:S(2)}) %collective-permute-start.6) | collective-permute-done | bytes 1048608 | tf_op jit(solution)/shard_map/ppermute | solution.py:39
  226.1 43.0 %collective-permute-done.7 = f32[512,512]{1,0:T(8,128)S(1)} collective-permute-done((f32[512,512]{1,0:T(8,128)S(1)}, f32[512,512]{1,0:T(8,128)S(1)}, u32[]{:S(2)}, u32[]{:S(2)}) %collective-permute-start.7) | collective-permute-done | bytes 1048608 | tf_op jit(solution)/shard_map/ppermute | solution.py:39
  271.1 35.7 %all-reduce.1 = (f32[]{:T(128)}, f32[]{:T(128)}) all-reduce(f32[]{:T(128)} %get-tuple-element.8, f32[]{:T(128)} %get-tuple-element.7), channel_id=1, replica_groups=mesh['sector'=8,'term'=4] {'sector'}, use_global_device_ids=true, to_apply=%region_7.0 | all-reduce | flops 2 | bytes 16 | tf_op jit(solution)/shard_map/psum | solution.py:40
  308.1 3.6 multiply_reduce_fusion.3
  311.7 12.4 %psum.68 = f32[]{:T(128)} all-reduce(f32[]{:T(128)} %get-tuple-element.20), channel_id=1, replica_groups=mesh['sector'=8,'term'=4] {'sector'}, use_global_device_ids=true, to_apply=%region_11.0 | all-reduce | flops 1 | bytes 8 | tf_op jit(solution)/shard_map/psum | solution.py:43
  329.4 4.1 collective-permute-done.8
  334.9 3.4 gather_fusion.2
  338.3 5.5 %fusion.44 = f32[512,512]{1,0:T(8,128)} fusion(bf16[4,1,512,512]{3,2,1,0:T(8,128)(2,1)S(1)} %copy-done, bf16[4,512,512]{2,1,0:T(8,128)(2,1)} %gather_fusion.2, bf16[4,1,512,512]{3,2,1,0:T(8,128)(2,1)} %param.6), kind=kOutput, calls=%fused_computation.26 | convolution fusion | flops 2148532224 | bytes 7340032 | tf_op jit(solution)/shard_map/tij,tkj->tik/dot_general | solution.py:21
  343.8 15.0 %collective-permute-done.10 = f32[512,512]{1,0:T(8,128)S(1)} collective-permute-done((f32[512,512]{1,0:T(8,128)}, f32[512,512]{1,0:T(8,128)S(1)}, u32[]{:S(2)}, u32[]{:S(2)}) %collective-permute-start.10) | collective-permute-done | bytes 1048608 | tf_op jit(solution)/shard_map/ppermute | solution.py:39
  361.6 44.4 %collective-permute-done.11 = f32[512,512]{1,0:T(8,128)} collective-permute-done((f32[512,512]{1,0:T(8,128)}, f32[512,512]{1,0:T(8,128)}, u32[]{:S(2)}, u32[]{:S(2)}) %collective-permute-start.11) | collective-permute-done | bytes 1048608 | tf_op jit(solution)/shard_map/ppermute | solution.py:39
  406.1 3.4 multiply_reduce_fusion.1
  409.5 34.6 %all-reduce = (f32[]{:T(128)}, f32[]{:T(128)}) all-reduce(f32[]{:T(128)} %get-tuple-element.6, f32[]{:T(128)} %get-tuple-element.5), channel_id=1, replica_groups=mesh['sector'=8,'term'=4] {'sector'}, use_global_device_ids=true, to_apply=%region_13.0 | all-reduce | flops 2 | bytes 16 | tf_op jit(solution)/shard_map/psum | solution.py:40
  445.4 3.5 multiply_reduce_fusion
  448.9 12.4 %psum.71 = f32[]{:T(128)} all-reduce(f32[]{:T(128)} %get-tuple-element.17), channel_id=1, replica_groups=mesh['sector'=8,'term'=4] {'sector'}, use_global_device_ids=true, to_apply=%region_17.0 | all-reduce | flops 1 | bytes 8 | tf_op jit(solution)/shard_map/psum | solution.py:43
  (45 shorter events, 41.6 us)
Async XLA Ops:
  6.5 48.4 %copy-start = (bf16[4,1,512,512]{3,2,1,0:T(8,128)(2,1)S(1)}, bf16[4,1,512,512]{3,2,1,0:T(8,128)(2,1)}, u32[]{:S(2)}) copy-start(bf16[4,1,512,512]{3,2,1,0:T(8,128)(2,1)} %param.7) | copy-start | bytes 6291460
  6.5 33.1 %all-gather.5.cloned.1.call-start = ((), (), s32[]{:S(2)}) async-start(), calls=%async_computation | async-start | bytes 1310720 | tf_op jit(solution)/shard_map/all_gather | solution.py:29
  7.3 168.2 %all-gather.7.cloned.1.call-start = ((), (), s32[]{:S(2)}) async-start(), calls=%async_computation.1 | async-start | bytes 1310720 | tf_op jit(solution)/shard_map/all_gather | solution.py:30
  39.6 6.3 %copy-start.2 = (f32[1,512,512]{2,1,0:T(8,128)S(1)}, f32[1,512,512]{2,1,0:T(8,128)}, u32[]{:S(2)}) copy-start(f32[1,512,512]{2,1,0:T(8,128)} %all-gather.5.cloned.1.call-done) | copy-start | bytes 3145732
  41.8 4.2 collective-permute-start.1
  43.9 5.0 %collective-permute-start = (bf16[512,512]{1,0:T(8,128)(2,1)}, bf16[512,512]{1,0:T(8,128)(2,1)}, u32[]{:S(2)}, u32[]{:S(2)}) collective-permute-start(bf16[512,512]{1,0:T(8,128)(2,1)} %bitcast_convert_fusion), channel_id=1, source_target_pairs={{4,0},{8,4},{12,8},{16,12},{20,16},{24,20},{28,24},{5,1},{9,5},{13... | collective-permute-start | bytes 1572872 | tf_op jit(solution)/shard_map/ppermute | solution.py:12
  60.5 17.3 %collective-permute-start.2 = (f32[512,512]{1,0:T(8,128)}, f32[512,512]{1,0:T(8,128)}, u32[]{:S(2)}, u32[]{:S(2)}) collective-permute-start(f32[512,512]{1,0:T(8,128)} %fusion.30), channel_id=1, source_target_pairs={{0,1},{1,0},{2,3},{3,2},{4,5},{5,4},{6,7},{7,6},{8,9},{9,8},{10,11... | collective-permute-start | bytes 3145736 | tf_op jit(solution)/shard_map/ppermute | solution.py:39
  79.5 56.7 %collective-permute-start.3 = (f32[512,512]{1,0:T(8,128)S(1)}, f32[512,512]{1,0:T(8,128)S(1)}, u32[]{:S(2)}, u32[]{:S(2)}) collective-permute-start(f32[512,512]{1,0:T(8,128)S(1)} %add.69), channel_id=1, source_target_pairs={{0,2},{1,3},{2,0},{3,1},{4,6},{5,7},{6,4},{7,5},{8,10},{9,11},{10,... | collective-permute-start | bytes 3145736 | tf_op jit(solution)/shard_map/ppermute | solution.py:39
  191.5 3.3 collective-permute-start.5
  193.3 5.6 %collective-permute-start.4 = (bf16[512,512]{1,0:T(8,128)(2,1)S(1)}, bf16[512,512]{1,0:T(8,128)(2,1)S(1)}, u32[]{:S(2)}, u32[]{:S(2)}) collective-permute-start(bf16[512,512]{1,0:T(8,128)(2,1)S(1)} %fusion.58), channel_id=1, source_target_pairs={{4,0},{8,4},{12,8},{16,12},{20,16},{24,20},{28,24},{5,1},{9,5},{13... | collective-permute-start | bytes 1572872 | tf_op jit(solution)/shard_map/ppermute | solution.py:12
  209.2 15.0 %collective-permute-start.6 = (f32[512,512]{1,0:T(8,128)}, f32[512,512]{1,0:T(8,128)S(1)}, u32[]{:S(2)}, u32[]{:S(2)}) collective-permute-start(f32[512,512]{1,0:T(8,128)} %fusion.37), channel_id=1, source_target_pairs={{0,1},{1,0},{2,3},{3,2},{4,5},{5,4},{6,7},{7,6},{8,9},{9,8},{10,11... | collective-permute-start | bytes 3145736 | tf_op jit(solution)/shard_map/ppermute | solution.py:39
  225.7 43.4 %collective-permute-start.7 = (f32[512,512]{1,0:T(8,128)S(1)}, f32[512,512]{1,0:T(8,128)S(1)}, u32[]{:S(2)}, u32[]{:S(2)}) collective-permute-start(f32[512,512]{1,0:T(8,128)S(1)} %add.72), channel_id=1, source_target_pairs={{0,2},{1,3},{2,0},{3,1},{4,6},{5,7},{6,4},{7,5},{8,10},{9,11},{10,... | collective-permute-start | bytes 3145736 | tf_op jit(solution)/shard_map/ppermute | solution.py:39
  311.7 17.6 %copy-start.1 = (f32[512,512]{1,0:T(8,128)S(1)}, f32[512,512]{1,0:T(8,128)}, u32[]{:S(2)}) copy-start(f32[512,512]{1,0:T(8,128)} %get-tuple-element.21) | copy-start | bytes 3145732
  326.1 3.3 collective-permute-start.9
  328.0 5.6 %collective-permute-start.8 = (bf16[512,512]{1,0:T(8,128)(2,1)S(1)}, bf16[512,512]{1,0:T(8,128)(2,1)S(1)}, u32[]{:S(2)}, u32[]{:S(2)}) collective-permute-start(bf16[512,512]{1,0:T(8,128)(2,1)S(1)} %fusion.59), channel_id=1, source_target_pairs={{4,0},{8,4},{12,8},{16,12},{20,16},{24,20},{28,24},{5,1},{9,5},{13... | collective-permute-start | bytes 1572872 | tf_op jit(solution)/shard_map/ppermute | solution.py:12
  343.8 15.0 %collective-permute-start.10 = (f32[512,512]{1,0:T(8,128)}, f32[512,512]{1,0:T(8,128)S(1)}, u32[]{:S(2)}, u32[]{:S(2)}) collective-permute-start(f32[512,512]{1,0:T(8,128)} %fusion.44), channel_id=1, source_target_pairs={{0,1},{1,0},{2,3},{3,2},{4,5},{5,4},{6,7},{7,6},{8,9},{9,8},{10,11... | collective-permute-start | bytes 3145736 | tf_op jit(solution)/shard_map/ppermute | solution.py:39
  361.3 44.8 %collective-permute-start.11 = (f32[512,512]{1,0:T(8,128)}, f32[512,512]{1,0:T(8,128)}, u32[]{:S(2)}, u32[]{:S(2)}) collective-permute-start(f32[512,512]{1,0:T(8,128)} %add.75), channel_id=1, source_target_pairs={{0,2},{1,3},{2,0},{3,1},{4,6},{5,7},{6,4},{7,5},{8,10},{9,11},{10,... | collective-permute-start | bytes 3145736 | tf_op jit(solution)/shard_map/ppermute | solution.py:39
Sparse Core Ops, SparseCore 0:
  8.9 30.6 all-gather.4
  62.0 47.4 all-gather.6
